TPU v7x, 32 devices: a whole 2x2x4 slice. The times are simulated.
32 devices in a mesh: band: 4 (over x, core), grid: 8 (over z, y).
Axes of the slice: x: 2, y: 2, z: 4, core: 2. Of those that a mesh axis runs over, the one named last changes fastest.
Arguments:
- orbitals: bfloat16 [16384, 2048], P('grid', 'band'), may hold values from -6 to 6
- projectors: bfloat16 [64, 8, 128], replicated, may hold values from -0.5 to 0.5
- sphere_start: int32 [64], replicated, may hold values from 0 to 1920, as said below
- proj_count: int32 [64], replicated, may hold values from 1 to 8
- owner_slab: int32 [64], replicated, may hold values from 0 to 7, as said below
- correlation_coef: float32 [64, 8, 8], replicated, as said below
Outputs:
- rotated: bfloat16 [16384, 2048], P(('grid', 'band'))
Inputs may be any that keep to these rules, and one draw needn't show every extreme that they name: `sphere_start`: a multiple of 128. `owner_slab`: every slab owns exactly 8 atoms. `correlation_coef`: each atom's matrix is symmetric positive definite.
All inputs are finite; a program needn't handle non-finite values.
Results may differ from a plain program's by a relative error of at most 0.0049.
Values may be sent and summed in bfloat16 or wider, within the bound.
A program may use at most 128 MiB of HBM per device.

v0:
```python
import jax
import jax.numpy as jnp
from jax import lax
from jax.sharding import PartitionSpec as P

SPH = 128
NPMAX = 8
A_SLAB = 8


def inverse_factor(matrix):
    order = matrix.shape[0]
    if order <= 512 or order % 2 != 0:
        lower = jnp.linalg.cholesky(matrix)
        identity = jnp.eye(order, dtype=matrix.dtype)
        return lax.linalg.triangular_solve(lower, identity, left_side=True, lower=True)
    half = order // 2
    upper_inv = inverse_factor(matrix[:half, :half])
    below = jnp.dot(matrix[half:, :half], upper_inv.T, precision=lax.Precision.HIGHEST)
    schur = matrix[half:, half:] - jnp.dot(below, below.T, precision=lax.Precision.HIGHEST)
    lower_inv = inverse_factor(schur)
    corner = -jnp.dot(
        lower_inv,
        jnp.dot(below, upper_inv, precision=lax.Precision.HIGHEST),
        precision=lax.Precision.HIGHEST,
    )
    top = jnp.concatenate([upper_inv, jnp.zeros((half, order - half), matrix.dtype)], axis=1)
    bottom = jnp.concatenate([corner, lower_inv], axis=1)
    return jnp.concatenate([top, bottom], axis=0)


def slab_atoms(owner_slab, slab):
    atoms = owner_slab.shape[0]
    keyed = jnp.where(owner_slab == slab, 0, 1) * atoms + jnp.arange(atoms, dtype=jnp.int32)
    return jnp.argsort(keyed, stable=True)[:A_SLAB]


def atom_terms(source, weights, starts, counts, coefs, valid):

    def take_rows(offset):
        return lax.dynamic_slice_in_dim(source, offset, SPH, 0)

    sphere_rows = jax.vmap(take_rows)(starts)
    correlations = jnp.einsum(
        "aij,ajn->ain", weights, sphere_rows, preferred_element_type=jnp.float32
    )
    active = (jnp.arange(NPMAX)[None, :] < counts[:, None]) & valid[:, None]
    correlations = jnp.where(active[:, :, None], correlations, jnp.zeros_like(correlations))
    weighted = jnp.einsum("aij,ajn->ain", coefs, correlations, precision=lax.Precision.HIGHEST)
    return (correlations, weighted)


def shards(orbitals, projectors, sphere_start, proj_count, owner_slab, correlation_coef):
    band_index = lax.axis_index("band")
    slab = lax.axis_index("grid")
    total_rows = orbitals.shape[0] * lax.axis_size("grid")
    chosen = slab_atoms(owner_slab, slab)
    weights = projectors[chosen]
    counts = proj_count[chosen]
    coefs = correlation_coef[chosen]
    mine = lax.all_to_all(orbitals, "band", split_axis=0, concat_axis=1, tiled=True)
    height = mine.shape[0]
    width_all = mine.shape[1]
    gram = jnp.dot(mine.T, mine, preferred_element_type=jnp.float32) * (1.0 / total_rows)
    offsets = sphere_start[chosen] - band_index * height
    valid = (offsets >= 0) & (offsets < height)
    offsets = jnp.clip(offsets, 0, height - SPH)
    correlations, weighted = atom_terms(mine, weights, offsets, counts, coefs, valid)
    paw = jnp.dot(
        weighted.reshape(-1, width_all).T,
        correlations.reshape(-1, width_all),
        precision=lax.Precision.HIGHEST,
    )
    metric = lax.psum(gram + paw, ("band", "grid"))
    inverse = inverse_factor(metric).astype(jnp.bfloat16)
    return jnp.dot(mine, inverse.T, preferred_element_type=jnp.float32).astype(jnp.bfloat16)


def solution(mesh):
    in_specs = (P("grid", "band"), P(), P(), P(), P(), P())
    out_specs = P(("grid", "band"), None)
    return jax.shard_map(shards, mesh=mesh, in_specs=in_specs, out_specs=out_specs, check_vma=False)
```

profile of v0, /device:TPU:0, one launch (start us, length us, event | category | flops | bytes accessed | tf_op | source)
XLA Modules:
  0.0 1109.8 jit_solution(1387231611529632680)
XLA Ops:
  16.0 21.5 %all-to-all-done = bf16[4,512,512]{2,1,0:T(8,128)(2,1)} async-done(((bf16[4,512,512]{2,1,0:T(8,128)(2,1)}), bf16[4,512,512]{2,1,0:T(8,128)(2,1)}, u32[]{:S(2)}, u32[]{:S(2)}) %all-to-all-start) | async-done | bytes 2097184 | tf_op jit(solution)/shard_map/all_to_all | solution.py:61
  40.3 20.2 %while.9 = (s32[]{:T(128)}, bf16[512,2048]{0,1:T(8,128)(2,1)S(1)}, s32[8,2]{0,1:T(2,128)S(1)}, bf16[8,128,2048]{2,1,0:T(8,128)(2,1)}, s32[]{:T(128)}) while((s32[]{:T(128)}, bf16[512,2048]{0,1:T(8,128)(2,1)S(1)}, s32[8,2]{0,1:T(2,128)S(1)}, bf16[8,128,2048]{2,1,0:T(8,128)(2,1)}, s32[]{:T(128)}) %tuple.122), condition=%wide.while_cond.1, body=%wide.while_body.1.sunk | while | flops 2 | bytes 3146333 | solution.py:41
  64.7 14.1 %fusion.178 = f32[2048,2048,1]{0,1,2:T(8,128)S(1)} fusion(f32[8,8,2048]{2,1,0:T(8,128)S(1)} %fusion.177, f32[8,8,2048]{2,1,0:T(8,128)S(1)} %convolution_select_fusion), kind=kOutput, calls=%fused_computation.329 | convolution fusion | flops 3221225472 | bytes 17825792 | tf_op jit(solution)/shard_map/dot_general | solution.py:69
  78.8 12.9 %bitcast_add_fusion = f32[2048,2048]{0,1:T(8,128)} fusion(f32[2048,2048,1]{0,1,2:T(8,128)S(1)} %fusion.178, bf16[512,2048]{0,1:T(8,128)(2,1)} %copy-done.4), kind=kOutput, calls=%fused_computation.16 | convolution fusion | flops 4303355904 | bytes 35651584 | tf_op jit(solution)/shard_map/dot_general | solution.py:64
  91.9 279.4 %all-reduce.7.cloned.1.call-done = f32[2048,2048]{0,1:T(8,128)} async-done(((f32[2048,2048]{0,1:T(8,128)}), f32[2048,2048]{0,1:T(8,128)}) %all-reduce.7.cloned.1.call-update) | async-done | bytes 16777232 | tf_op jit(solution)/shard_map/psum | solution.py:74
  374.4 11.7 %cholesky.462 = f32[128,128]{1,0:T(8,128)S(1)} custom-call(f32[128,128]{1,0:T(8,128)S(1)} %cholesky.746), custom_call_target="Cholesky" | custom-call | tf_op jit(solution)/shard_map/jit(cholesky)/cholesky | solution.py:14
  386.1 9.9 custom-call.35
  396.9 11.7 %cholesky.481 = f32[128,128]{1,0:T(8,128)S(1)} custom-call(f32[128,128]{1,0:T(8,128)S(1)} %cholesky.750), custom_call_target="Cholesky" | custom-call | tf_op jit(solution)/shard_map/jit(cholesky)/cholesky | solution.py:14
  408.6 9.8 custom-call.36
  419.1 11.9 %cholesky.502 = f32[128,128]{1,0:T(8,128)S(1)} custom-call(f32[128,128]{1,0:T(8,128)S(1)} %cholesky.755), custom_call_target="Cholesky" | custom-call | tf_op jit(solution)/shard_map/jit(cholesky)/cholesky | solution.py:14
  431.7 9.8 custom-call.37
  442.1 11.7 %cholesky.519 = f32[128,128]{1,0:T(8,128)S(1)} custom-call(f32[128,128]{1,0:T(8,128)S(1)} %convolution_subtract_fusion.25), custom_call_target="Cholesky" | custom-call | tf_op jit(solution)/shard_map/jit(cholesky)/cholesky | solution.py:14
  457.9 8.1 while.10
  466.0 39.7 %custom-call.38 = f32[4,128,128]{1,2,0:T(8,128)S(1)} custom-call(f32[4,128,128]{2,1,0:T(8,128)S(1)} %get-tuple-element.43), custom_call_target="InvertDiagBlocksLowerTriangular" | custom-call | tf_op jit(solution)/shard_map/triangular_solve/custom-call.3 | solution.py:16
  523.4 11.9 %cholesky.534 = f32[128,128]{1,0:T(8,128)S(1)} custom-call(f32[128,128]{1,0:T(8,128)S(1)} %cholesky.759), custom_call_target="Cholesky" | custom-call | tf_op jit(solution)/shard_map/jit(cholesky)/cholesky | solution.py:14
  535.5 9.8 custom-call.39
  547.8 11.7 %cholesky.553 = f32[128,128]{1,0:T(8,128)S(1)} custom-call(f32[128,128]{1,0:T(8,128)S(1)} %cholesky.763), custom_call_target="Cholesky" | custom-call | tf_op jit(solution)/shard_map/jit(cholesky)/cholesky | solution.py:14
  560.9 9.8 custom-call.40
  572.3 12.1 %cholesky.574 = f32[128,128]{1,0:T(8,128)S(1)} custom-call(f32[128,128]{1,0:T(8,128)S(1)} %cholesky.768), custom_call_target="Cholesky" | custom-call | tf_op jit(solution)/shard_map/jit(cholesky)/cholesky | solution.py:14
  585.1 9.8 custom-call.41
  596.4 11.7 %cholesky.591 = f32[128,128]{1,0:T(8,128)S(1)} custom-call(f32[128,128]{1,0:T(8,128)S(1)} %convolution_subtract_fusion.24), custom_call_target="Cholesky" | custom-call | tf_op jit(solution)/shard_map/jit(cholesky)/cholesky | solution.py:14
  612.4 11.7 %while.11 = (s32[]{:T(128)}, f32[512,512]{1,0:T(8,128)}, s32[4,2]{0,1:T(2,128)S(1)}, f32[4,128,128]{2,1,0:T(8,128)S(1)}, s32[]{:T(128)}) while((s32[]{:T(128)}, f32[512,512]{1,0:T(8,128)}, s32[4,2]{0,1:T(2,128)S(1)}, f32[4,128,128]{2,1,0:T(8,128)S(1)}, s32[]{:T(128)}) %tuple.123), condition=%wide.while_cond.clone, body=%wide.while_body.clone.sunk | while | flops 2 | bytes 131181 | solution.py:16
  624.0 39.3 %custom-call.42 = f32[4,128,128]{1,2,0:T(8,128)S(1)} custom-call(f32[4,128,128]{2,1,0:T(8,128)S(1)} %get-tuple-element.44), custom_call_target="InvertDiagBlocksLowerTriangular" | custom-call | tf_op jit(solution)/shard_map/triangular_solve/custom-call.3 | solution.py:16
  672.0 28.8 %fusion.9 = f32[1024,1024]{1,0:T(8,128)S(1)} fusion(f32[2048,2048]{0,1:T(8,128)} %all-reduce.7.cloned.1.call-done, f32[512,512]{1,0:T(8,128)S(1)} %copy-done.9, f32[128,512]{1,0:T(8,128)S(1)} %fusion.126, f32[128,512]{1,0:T(8,128)S(1)} %fusion.127, f32[128,512]{1,0:T(8,128)S(1)} %fusion.129, f32[128,512]{1,0:T(8,128)S(1)} %fusion.82, ...), kind=kOutput, calls=%fused_computation.26 | convolution fusion | flops 12892241920 | bytes 11534336 | tf_op jit(solution)/shard_map/dot_general | solution.py:19
  700.9 16.8 %fusion.171 = f32[1024,1024]{1,0:T(8,128)} fusion(f32[1024,1024]{1,0:T(8,128)S(1)} %fusion.9, f32[512,512]{1,0:T(8,128)S(1)} %copy-done.9, f32[128,512]{1,0:T(8,128)S(1)} %fusion.126, f32[128,512]{1,0:T(8,128)S(1)} %fusion.127, f32[128,512]{1,0:T(8,128)S(1)} %fusion.129, f32[128,512]{1,0:T(8,128)S(1)} %fusion.82, f32[512,512]{1,0:T(8,128)S(1)} %convolution_negate_fusion.1), kind=kOutput, calls=%fused_computation.322 | convolution fusion | flops 12892241920 | bytes 11534336 | tf_op jit(solution)/shard_map/dot_general | solution.py:24
  717.7 15.8 %slice_subtract_fusion = f32[1024,1024]{0,1:T(8,128)S(1)} fusion(f32[2048,2048]{0,1:T(8,128)} %all-reduce.7.cloned.1.call-done, f32[1024,1024]{1,0:T(8,128)S(1)} %fusion.9), kind=kOutput, calls=%fused_computation.28 | convolution fusion | flops 12885950464 | bytes 16777216 | tf_op jit(solution)/shard_map/dot_general | solution.py:20
  740.4 11.7 %cholesky.606 = f32[128,128]{1,0:T(8,128)S(1)} custom-call(f32[128,128]{1,0:T(8,128)S(1)} %cholesky.772), custom_call_target="Cholesky" | custom-call | tf_op jit(solution)/shard_map/jit(cholesky)/cholesky | solution.py:14
  752.3 9.8 custom-call.43
  764.7 11.7 %cholesky.625 = f32[128,128]{1,0:T(8,128)S(1)} custom-call(f32[128,128]{1,0:T(8,128)S(1)} %cholesky.776), custom_call_target="Cholesky" | custom-call | tf_op jit(solution)/shard_map/jit(cholesky)/cholesky | solution.py:14
  777.8 10.2 custom-call.44
  789.5 11.7 %cholesky.646 = f32[128,128]{1,0:T(8,128)S(1)} custom-call(f32[128,128]{1,0:T(8,128)S(1)} %cholesky.781), custom_call_target="Cholesky" | custom-call | tf_op jit(solution)/shard_map/jit(cholesky)/cholesky | solution.py:14
  802.0 9.8 custom-call.45
  813.2 11.7 %cholesky.663 = f32[128,128]{1,0:T(8,128)S(1)} custom-call(f32[128,128]{1,0:T(8,128)S(1)} %convolution_subtract_fusion.23), custom_call_target="Cholesky" | custom-call | tf_op jit(solution)/shard_map/jit(cholesky)/cholesky | solution.py:14
  829.4 11.7 %while.12 = (s32[]{:T(128)}, f32[512,512]{1,0:T(8,128)}, s32[4,2]{0,1:T(2,128)S(1)}, f32[4,128,128]{2,1,0:T(8,128)S(1)}, s32[]{:T(128)}) while((s32[]{:T(128)}, f32[512,512]{1,0:T(8,128)}, s32[4,2]{0,1:T(2,128)S(1)}, f32[4,128,128]{2,1,0:T(8,128)S(1)}, s32[]{:T(128)}) %tuple.124), condition=%wide.while_cond.clone.1, body=%wide.while_body.clone.1.sunk | while | flops 2 | bytes 131181 | solution.py:16
  841.0 39.3 %custom-call.46 = f32[4,128,128]{1,2,0:T(8,128)S(1)} custom-call(f32[4,128,128]{2,1,0:T(8,128)S(1)} %get-tuple-element.45), custom_call_target="InvertDiagBlocksLowerTriangular" | custom-call | tf_op jit(solution)/shard_map/triangular_solve/custom-call.3 | solution.py:16
  895.8 7.4 fusion.172
  907.0 11.7 %cholesky.678 = f32[128,128]{1,0:T(8,128)S(1)} custom-call(f32[128,128]{1,0:T(8,128)S(1)} %cholesky.785), custom_call_target="Cholesky" | custom-call | tf_op jit(solution)/shard_map/jit(cholesky)/cholesky | solution.py:14
  918.8 9.8 custom-call.47
  931.2 11.7 %cholesky.697 = f32[128,128]{1,0:T(8,128)S(1)} custom-call(f32[128,128]{1,0:T(8,128)S(1)} %cholesky.789), custom_call_target="Cholesky" | custom-call | tf_op jit(solution)/shard_map/jit(cholesky)/cholesky | solution.py:14
  944.3 10.0 custom-call.48
  955.8 11.7 %cholesky.718 = f32[128,128]{1,0:T(8,128)S(1)} custom-call(f32[128,128]{1,0:T(8,128)S(1)} %cholesky.794), custom_call_target="Cholesky" | custom-call | tf_op jit(solution)/shard_map/jit(cholesky)/cholesky | solution.py:14
  968.3 9.8 custom-call.49
  979.5 11.7 %cholesky.735 = f32[128,128]{1,0:T(8,128)S(1)} custom-call(f32[128,128]{1,0:T(8,128)S(1)} %convolution_subtract_fusion.22), custom_call_target="Cholesky" | custom-call | tf_op jit(solution)/shard_map/jit(cholesky)/cholesky | solution.py:14
  995.8 11.7 %while.13 = (s32[]{:T(128)}, f32[512,512]{1,0:T(8,128)}, s32[4,2]{0,1:T(2,128)S(1)}, f32[4,128,128]{2,1,0:T(8,128)S(1)}, s32[]{:T(128)}) while((s32[]{:T(128)}, f32[512,512]{1,0:T(8,128)}, s32[4,2]{0,1:T(2,128)S(1)}, f32[4,128,128]{2,1,0:T(8,128)S(1)}, s32[]{:T(128)}) %tuple.125), condition=%wide.while_cond.clone.2, body=%wide.while_body.clone.2.sunk | while | flops 2 | bytes 131181 | solution.py:16
  1007.5 39.3 %custom-call.50 = f32[4,128,128]{1,2,0:T(8,128)S(1)} custom-call(f32[4,128,128]{2,1,0:T(8,128)S(1)} %get-tuple-element.46), custom_call_target="InvertDiagBlocksLowerTriangular" | custom-call | tf_op jit(solution)/shard_map/triangular_solve/custom-call.3 | solution.py:16
  1054.6 6.0 fusion.18
  1060.6 13.6 %negate_convert_fusion = bf16[1024,1024]{1,0:T(8,128)(2,1)S(1)} fusion(f32[1024,1024]{1,0:T(8,128)S(1)} %copy-done.23, f32[512,512]{1,0:T(8,128)S(1)} %copy-done.11, f32[128,512]{1,0:T(8,128)S(1)} %fusion.114, f32[128,512]{1,0:T(8,128)S(1)} %fusion.115, f32[128,512]{1,0:T(8,128)S(1)} %fusion.117, f32[128,512]{1,0:T(8,128)S(1)} %fusion.78, ...), kind=kOutput, calls=%fused_computation.32 | convolution fusion | flops 12894339072 | bytes 9437184 | tf_op jit(solution)/shard_map/dot_general | solution.py:22
  1074.3 25.8 %fusion.15 = bf16[512,2048]{0,1:T(8,128)(2,1)S(1)} fusion(bf16[512,2048]{0,1:T(8,128)(2,1)S(1)} %copy-done.5, bf16[1024,1024]{1,0:T(8,128)(2,1)S(1)} %copy-done.19, bf16[1024,1024]{1,0:T(8,128)(2,1)S(1)} %fusion.18, bf16[1024,1024]{1,0:T(8,128)(2,1)S(1)} %negate_convert_fusion), kind=kOutput, calls=%fused_computation.34 | convolution fusion | flops 4329570304 | bytes 10485760 | tf_op jit(solution)/shard_map/dot_general | solution.py:76
  (288 shorter events, 177.9 us)
Async XLA Ops:
  6.5 8.1 copy-start
  6.5 4.7 copy-start.22
  6.5 6.8 copy-start.2
  6.5 7.4 copy-start.3
  6.5 8.7 copy-start.21
  6.5 31.0 %all-to-all-start = ((bf16[4,512,512]{2,1,0:T(8,128)(2,1)}), bf16[4,512,512]{2,1,0:T(8,128)(2,1)}, u32[]{:S(2)}, u32[]{:S(2)}) async-start(bf16[4,512,512]{2,1,0:T(8,128)(2,1)} %bitcast.231), calls=%async_computation | async-start | bytes 4194304 | tf_op jit(solution)/shard_map/all_to_all | solution.py:61
  11.1 360.1 %all-reduce.7.cloned.1.call-start = ((), (), s32[]{:S(2)}) async-start(), calls=%async_computation.1 | async-start | bytes 33554432 | tf_op jit(solution)/shard_map/psum | solution.py:74
  60.5 3.6 copy-start.4
  522.4 1.0 copy-start.14
  663.4 3.5 copy-start.20
  663.8 8.2 copy-start.9
  670.1 30.7 %copy-start.17 = (f32[128,512]{1,0:T(8,128)}, f32[128,512]{1,0:T(8,128)S(1)}, u32[]{:S(2)}) copy-start(f32[128,512]{1,0:T(8,128)S(1)} %fusion.126) | copy-start | bytes 786436
  672.0 28.9 %copy-start.6 = (f32[512,512]{1,0:T(8,128)}, f32[512,512]{1,0:T(8,128)S(1)}, u32[]{:S(2)}) copy-start(f32[512,512]{1,0:T(8,128)S(1)} %convolution_negate_fusion.1) | copy-start | bytes 3145732
  733.5 1.9 copy-start.12
  739.5 1.0 copy-start.16
  880.3 7.1 copy-start.13
  891.0 4.8 copy-start.7
  891.0 4.8 copy-start.10
  891.0 4.8 copy-start.18
  906.0 1.0 copy-start.15
  994.4 58.3 %copy-start.8 = (f32[512,512]{1,0:T(8,128)S(1)}, f32[512,512]{1,0:T(8,128)}, u32[]{:S(2)}) copy-start(f32[512,512]{1,0:T(8,128)} %fusion.169) | copy-start | bytes 3145732
  1047.2 7.4 copy-start.11
  1052.7 7.9 copy-start.23
  1060.6 13.7 %copy-start.5 = (bf16[512,2048]{0,1:T(8,128)(2,1)S(1)}, bf16[512,2048]{0,1:T(8,128)(2,1)}, u32[]{:S(2)}) copy-start(bf16[512,2048]{0,1:T(8,128)(2,1)} %copy-done.4) | copy-start | bytes 6291460
  1060.6 13.7 %copy-start.19 = (bf16[1024,1024]{1,0:T(8,128)(2,1)S(1)}, bf16[1024,1024]{1,0:T(8,128)(2,1)}, u32[]{:S(2)}) copy-start(bf16[1024,1024]{1,0:T(8,128)(2,1)} %fusion.172) | copy-start | bytes 6291460
  1074.3 28.2 %copy-start.1 = (bf16[64,8,128]{2,1,0:T(8,128)(2,1)S(1)}, bf16[64,8,128]{2,1,0:T(8,128)(2,1)}, u32[]{:S(2)}) copy-start(bf16[64,8,128]{2,1,0:T(8,128)(2,1)} %param.10) | copy-start | bytes 393220
Sparse Core Ops, SparseCore 0:
  91.8 279.3 all-reduce.6
where the time goes:
time: 1120 us; the launch traced here: 1110 us
  other arithmetic  502 us (45%)
  waiting for transfers between devices  301 us (27%)
  matrix products  194 us (17%)
  local copies, waits for them, and re-layouts  83.1 us (7%)
  between operations  25.2 us (2%)
    another operation x59, other arithmetic, inverse_factor(): lower = jnp.linalg.cholesky(matrix)  317 us
    psum x1, waiting for transfers between devices, shards(): metric = lax.psum(gram + paw, ('band', 'grid'))  279 us
    another operation x11, other arithmetic, inverse_factor(): lax.linalg.triangular_solve(lower, identity, left_side=True, lower=True)  163 us
    another operation x53, local copies, waits for them, and re-layouts, inverse_factor(): lax.linalg.triangular_solve(lower, identity, left_side=True, lower=True)  42.9 us
    dot_general x3, matrix products, inverse_factor(): jnp.dot(matrix[half:, :half], upper_inv.T, precision=lax.Precision.HIGHEST)  37.1 us
    dot_general x1, matrix products, shards(): jnp.dot(mine, inverse.T, preferred_element_type=jnp.float32)  25.8 us
  transfers between devices with their start and end apart: 2, of which 2 were waited for; matrix products, arithmetic and copies ran while one was open for 0% of the time, Pallas kernels for 0%

commit v1 on v0

--- a/solution.py
+++ b/solution.py
@@ -71,7 +71,8 @@
         correlations.reshape(-1, width_all),
         precision=lax.Precision.HIGHEST,
     )
-    metric = lax.psum(gram + paw, ("band", "grid"))
+    one_axis = lax.psum(gram + paw, "grid")
+    metric = lax.psum(one_axis, "band")
     inverse = inverse_factor(metric).astype(jnp.bfloat16)
     return jnp.dot(mine, inverse.T, preferred_element_type=jnp.float32).astype(jnp.bfloat16)
 

time: 1120 us -> 1640 us (1.46)
  waiting for transfers between devices: 301 us -> 822 us
    psum x1 -> x2, waiting for transfers between devices: 279 us -> 801 us  [the longest x1 511 us: shards(): one_axis = lax.psum(gram + paw, 'grid')]
  transfers between devices with their start and end apart: 2 -> 3, of which waited for: 2 -> 3; matrix products, arithmetic and copies ran while one was open for 0% -> 0% of each run, Pallas kernels for 0% -> 0%
where the time goes in v1:
time: 1640 us; the launch traced here: 1630 us
  waiting for transfers between devices  822 us (50%)
  other arithmetic  502 us (31%)
  matrix products  194 us (12%)
  local copies, waits for them, and re-layouts  83.1 us (5%)
  between operations  25.2 us (2%)
    psum x1, waiting for transfers between devices, shards(): one_axis = lax.psum(gram + paw, 'grid')  511 us
    another operation x59, other arithmetic, inverse_factor(): lower = jnp.linalg.cholesky(matrix)  317 us
    psum x1, waiting for transfers between devices, shards(): metric = lax.psum(one_axis, 'band')  290 us
    another operation x11, other arithmetic, inverse_factor(): lax.linalg.triangular_solve(lower, identity, left_side=True, lower=True)  163 us
    another operation x53, local copies, waits for them, and re-layouts, inverse_factor(): lax.linalg.triangular_solve(lower, identity, left_side=True, lower=True)  42.9 us
    dot_general x3, matrix products, inverse_factor(): jnp.dot(matrix[half:, :half], upper_inv.T, precision=lax.Precision.HIGHEST)  37.1 us
  transfers between devices with their start and end apart: 3, of which 3 were waited for; matrix products, arithmetic and copies ran while one was open for 0% of the time, Pallas kernels for 0%

profile of v1, /device:TPU:0, one launch (start us, length us, event | category | flops | bytes accessed | tf_op | source)
XLA Modules:
  0.0 1631.0 jit_solution(15490862944175929372)
XLA Ops:
  16.0 21.5 %all-to-all-done = bf16[4,512,512]{2,1,0:T(8,128)(2,1)} async-done(((bf16[4,512,512]{2,1,0:T(8,128)(2,1)}), bf16[4,512,512]{2,1,0:T(8,128)(2,1)}, u32[]{:S(2)}, u32[]{:S(2)}) %all-to-all-start) | async-done | bytes 2097184 | tf_op jit(solution)/shard_map/all_to_all | solution.py:61
  40.3 20.2 %while.9 = (s32[]{:T(128)}, bf16[512,2048]{0,1:T(8,128)(2,1)S(1)}, s32[8,2]{0,1:T(2,128)S(1)}, bf16[8,128,2048]{2,1,0:T(8,128)(2,1)}, s32[]{:T(128)}) while((s32[]{:T(128)}, bf16[512,2048]{0,1:T(8,128)(2,1)S(1)}, s32[8,2]{0,1:T(2,128)S(1)}, bf16[8,128,2048]{2,1,0:T(8,128)(2,1)}, s32[]{:T(128)}) %tuple.124), condition=%wide.while_cond.1, body=%wide.while_body.1.sunk | while | flops 2 | bytes 3146333 | solution.py:41
  64.7 14.1 fusion.178
  78.8 12.9 bitcast_add_fusion
  91.8 511.0 %all-reduce.8.cloned.1.call-done = f32[2048,2048]{0,1:T(8,128)} async-done(((f32[2048,2048]{0,1:T(8,128)}), f32[2048,2048]{0,1:T(8,128)}) %all-reduce.8.cloned.1.call-update) | async-done | bytes 16777232 | tf_op jit(solution)/shard_map/psum | solution.py:74
  602.9 289.7 %all-reduce.10.cloned.1.call-done = f32[2048,2048]{0,1:T(8,128)} async-done(((f32[2048,2048]{0,1:T(8,128)}), f32[2048,2048]{0,1:T(8,128)}) %all-reduce.10.cloned.1.call-update) | async-done | bytes 16777232 | tf_op jit(solution)/shard_map/psum | solution.py:75
  895.8 11.7 cholesky.462
  907.5 9.8 custom-call.35
  918.1 11.7 cholesky.481
  929.9 10.0 custom-call.36
  940.5 11.7 cholesky.502
  952.9 9.8 custom-call.37
  963.3 11.7 cholesky.519
  979.5 8.1 while.10
  987.6 39.3 %custom-call.38 = f32[4,128,128]{1,2,0:T(8,128)S(1)} custom-call(f32[4,128,128]{2,1,0:T(8,128)S(1)} %get-tuple-element.43), custom_call_target="InvertDiagBlocksLowerTriangular" | custom-call | tf_op jit(solution)/shard_map/triangular_solve/custom-call.3 | solution.py:16
  1044.7 11.9 cholesky.534
  1056.7 9.8 custom-call.39
  1069.0 11.7 cholesky.553
  1082.1 9.8 custom-call.40
  1093.5 12.1 cholesky.574
  1106.4 9.8 custom-call.41
  1117.6 11.7 cholesky.591
  1133.6 11.7 while.11
  1145.3 39.3 %custom-call.42 = f32[4,128,128]{1,2,0:T(8,128)S(1)} custom-call(f32[4,128,128]{2,1,0:T(8,128)S(1)} %get-tuple-element.44), custom_call_target="InvertDiagBlocksLowerTriangular" | custom-call | tf_op jit(solution)/shard_map/triangular_solve/custom-call.3 | solution.py:16
  1193.2 28.8 %fusion.9 = f32[1024,1024]{1,0:T(8,128)S(1)} fusion(f32[2048,2048]{0,1:T(8,128)} %all-reduce.10.cloned.1.call-done, f32[512,512]{1,0:T(8,128)S(1)} %copy-done.9, f32[128,512]{1,0:T(8,128)S(1)} %fusion.126, f32[128,512]{1,0:T(8,128)S(1)} %fusion.127, f32[128,512]{1,0:T(8,128)S(1)} %fusion.129, f32[128,512]{1,0:T(8,128)S(1)} %fusion.82, ...), kind=kOutput, calls=%fused_computation.26 | convolution fusion | flops 12892241920 | bytes 11534336 | tf_op jit(solution)/shard_map/dot_general | solution.py:19
  1222.1 16.8 %fusion.171 = f32[1024,1024]{1,0:T(8,128)} fusion(f32[1024,1024]{1,0:T(8,128)S(1)} %fusion.9, f32[512,512]{1,0:T(8,128)S(1)} %copy-done.9, f32[128,512]{1,0:T(8,128)S(1)} %fusion.126, f32[128,512]{1,0:T(8,128)S(1)} %fusion.127, f32[128,512]{1,0:T(8,128)S(1)} %fusion.129, f32[128,512]{1,0:T(8,128)S(1)} %fusion.82, f32[512,512]{1,0:T(8,128)S(1)} %convolution_negate_fusion.1), kind=kOutput, calls=%fused_computation.322 | convolution fusion | flops 12892241920 | bytes 11534336 | tf_op jit(solution)/shard_map/dot_general | solution.py:24
  1238.9 15.8 slice_subtract_fusion
  1261.7 11.7 cholesky.606
  1273.5 9.8 custom-call.43
  1285.9 11.7 cholesky.625
  1299.0 10.2 custom-call.44
  1310.8 11.7 cholesky.646
  1323.2 9.8 custom-call.45
  1334.4 11.7 cholesky.663
  1350.6 11.7 while.12
  1362.2 39.3 %custom-call.46 = f32[4,128,128]{1,2,0:T(8,128)S(1)} custom-call(f32[4,128,128]{2,1,0:T(8,128)S(1)} %get-tuple-element.45), custom_call_target="InvertDiagBlocksLowerTriangular" | custom-call | tf_op jit(solution)/shard_map/triangular_solve/custom-call.3 | solution.py:16
  1417.0 7.4 fusion.172
  1428.2 11.7 cholesky.678
  1440.1 9.8 custom-call.47
  1452.4 11.7 cholesky.697
  1465.5 10.0 custom-call.48
  1477.0 11.7 cholesky.718
  1489.5 9.8 custom-call.49
  1500.8 11.7 cholesky.735
  1517.0 11.7 while.13
  1528.7 39.3 %custom-call.50 = f32[4,128,128]{1,2,0:T(8,128)S(1)} custom-call(f32[4,128,128]{2,1,0:T(8,128)S(1)} %get-tuple-element.46), custom_call_target="InvertDiagBlocksLowerTriangular" | custom-call | tf_op jit(solution)/shard_map/triangular_solve/custom-call.3 | solution.py:16
  1581.8 13.6 negate_convert_fusion
  1595.5 25.8 %fusion.15 = bf16[512,2048]{0,1:T(8,128)(2,1)S(1)} fusion(bf16[512,2048]{0,1:T(8,128)(2,1)S(1)} %copy-done.5, bf16[1024,1024]{1,0:T(8,128)(2,1)S(1)} %copy-done.19, bf16[1024,1024]{1,0:T(8,128)(2,1)S(1)} %fusion.18, bf16[1024,1024]{1,0:T(8,128)(2,1)S(1)} %negate_convert_fusion), kind=kOutput, calls=%fused_computation.34 | convolution fusion | flops 4329570304 | bytes 10485760 | tf_op jit(solution)/shard_map/dot_general | solution.py:77
  (291 shorter events, 184.4 us)
Async XLA Ops:
  6.5 8.1 copy-start
  6.5 4.7 copy-start.22
  6.5 6.8 copy-start.2
  6.5 7.4 copy-start.3
  6.5 8.7 copy-start.21
  6.5 31.0 %all-to-all-start = ((bf16[4,512,512]{2,1,0:T(8,128)(2,1)}), bf16[4,512,512]{2,1,0:T(8,128)(2,1)}, u32[]{:S(2)}, u32[]{:S(2)}) async-start(bf16[4,512,512]{2,1,0:T(8,128)(2,1)} %bitcast.231), calls=%async_computation | async-start | bytes 4194304 | tf_op jit(solution)/shard_map/all_to_all | solution.py:61
  11.1 591.6 %all-reduce.8.cloned.1.call-start = ((), (), s32[]{:S(2)}) async-start(), calls=%async_computation.1 | async-start | bytes 33554432 | tf_op jit(solution)/shard_map/psum | solution.py:74
  60.5 3.6 copy-start.4
  91.7 800.9 %all-reduce.10.cloned.1.call-start = ((), (), s32[]{:S(2)}) async-start(), calls=%async_computation.2 | async-start | bytes 33554432 | tf_op jit(solution)/shard_map/psum | solution.py:75
  1043.6 1.0 copy-start.14
  1184.6 3.5 copy-start.20
  1185.0 8.2 copy-start.9
  1191.4 30.7 %copy-start.17 = (f32[128,512]{1,0:T(8,128)}, f32[128,512]{1,0:T(8,128)S(1)}, u32[]{:S(2)}) copy-start(f32[128,512]{1,0:T(8,128)S(1)} %fusion.126) | copy-start | bytes 786436
  1193.2 28.9 %copy-start.6 = (f32[512,512]{1,0:T(8,128)}, f32[512,512]{1,0:T(8,128)S(1)}, u32[]{:S(2)}) copy-start(f32[512,512]{1,0:T(8,128)S(1)} %convolution_negate_fusion.1) | copy-start | bytes 3145732
  1254.7 1.9 copy-start.12
  1260.7 1.0 copy-start.16
  1401.6 7.1 copy-start.13
  1412.2 4.8 copy-start.7
  1412.2 4.8 copy-start.10
  1412.3 4.8 copy-start.18
  1427.2 1.0 copy-start.15
  1515.6 58.3 %copy-start.8 = (f32[512,512]{1,0:T(8,128)S(1)}, f32[512,512]{1,0:T(8,128)}, u32[]{:S(2)}) copy-start(f32[512,512]{1,0:T(8,128)} %fusion.169) | copy-start | bytes 3145732
  1568.4 7.4 copy-start.11
  1574.0 7.9 copy-start.23
  1581.8 13.7 copy-start.5
  1581.8 13.7 copy-start.19
  1595.5 28.2 %copy-start.1 = (bf16[64,8,128]{2,1,0:T(8,128)(2,1)S(1)}, bf16[64,8,128]{2,1,0:T(8,128)(2,1)}, u32[]{:S(2)}) copy-start(bf16[64,8,128]{2,1,0:T(8,128)(2,1)} %param.10) | copy-start | bytes 393220
Sparse Core Ops, SparseCore 0:
  91.8 510.8 all-reduce.7
  605.3 287.3 all-reduce.9
